TPU v7x, 32 devices: a whole 2x2x4 slice. The times are simulated.
32 devices in a mesh: row: 8 (over z, x), col: 4 (over y, core).
Axes of the slice: x: 2, y: 2, z: 4, core: 2. Of those that a mesh axis runs over, the one named last changes fastest.
Arguments:
- hamiltonian: bfloat16 [2, 2048, 2048], P(None, 'row', 'col'), may hold values from -0.25 to 0.25
- basis_metric: bfloat16 [2048, 2048], P('row', 'col'), may hold values from -0.25 to 0.25
- density: bfloat16 [2, 2048, 2048], P(None, 'row', 'col'), may hold values from -6 to 6
- hamiltonian_keep: int32 [16, 16], P('row', 'col'), may hold values from 0 to 1, as said below
- metric_keep: int32 [16, 16], P('row', 'col'), may hold values from 0 to 1, as said below
- density_keep: int32 [16, 16], P('row', 'col'), may hold values from 0 to 1, as said below
- gradient_keep: int32 [16, 16], P('row', 'col'), may hold values 0 or 1
Outputs:
- gradient: float32 [2, 2048, 2048], P(None, 'row', 'col')
Inputs may be any that keep to these rules, and one draw needn't show every extreme that they name: `hamiltonian_keep`: each block row has at most 4 blocks in the pattern, and some rows have exactly 4. `metric_keep`: each block row has at most 4 blocks in the pattern, and some rows have exactly 4. `density_keep`: each block row keeps at most 7 blocks, and some rows keep exactly 7.
All inputs are finite; a program needn't handle non-finite values. No bound on the sum of `gradient_keep` on one device may be relied on, other than what follows from the above.
Results may differ from a plain program's by a relative error of at most 0.0029.
Values may be sent and summed in bfloat16 or wider, within the bound.
No kernel may reach another device: no remote copies, remote signals or barrier semaphores. Data moves between devices by JAX's collectives and lax.ppermute only.
A program may use at most 64 MiB of HBM per device.

v0:
```python
import jax
import jax.numpy as jnp
from jax import lax
from jax.sharding import PartitionSpec as P

BLOCK = 128


def widen(keep):
    return jnp.repeat(jnp.repeat(keep, BLOCK, axis=0), BLOCK, axis=1) > 0


def first_terms(rows_part, cols_part):
    hterm = jnp.einsum("srl,slc->src", rows_part[:2], cols_part, preferred_element_type=jnp.float32)
    sterm = jnp.einsum("rl,slc->src", rows_part[2], cols_part, preferred_element_type=jnp.float32)
    return jnp.concatenate([hterm, sterm], axis=0)


def second_terms(rows_part, cols_part):
    left = jnp.einsum(
        "srl,lc->src", rows_part[:2], cols_part[2], preferred_element_type=jnp.float32
    )
    right = jnp.einsum(
        "srl,slc->src", rows_part[2:], cols_part[:2], preferred_element_type=jnp.float32
    )
    return left - right


def body(
    hamiltonian, basis_metric, density, hamiltonian_keep, metric_keep, density_keep, gradient_keep
):
    kohn_sham = jnp.where(widen(hamiltonian_keep)[None], hamiltonian, jnp.zeros_like(hamiltonian))
    smat = jnp.where(widen(metric_keep), basis_metric, jnp.zeros_like(basis_metric))
    filtered = jnp.where(widen(density_keep)[None], density, jnp.zeros_like(density))
    operators = jnp.concatenate([kohn_sham, smat[None]], axis=0)
    density_cols = lax.all_gather(filtered, "row", axis=1, tiled=True)
    cols_part = density_cols
    products = first_terms(lax.all_gather(operators, "col", axis=2, tiled=True), cols_part)
    products = products.astype(jnp.bfloat16)
    operator_cols = lax.all_gather(operators, "row", axis=1, tiled=True)
    cols_part = operator_cols
    commut = second_terms(lax.all_gather(products, "col", axis=2, tiled=True), cols_part)
    grad_mask = widen(gradient_keep)[None]
    return jnp.where(grad_mask, commut, jnp.zeros_like(commut))


def solution(mesh):
    in_specs = (
        P(None, "row", "col"),
        P("row", "col"),
        P(None, "row", "col"),
        P("row", "col"),
        P("row", "col"),
        P("row", "col"),
        P("row", "col"),
    )
    out_specs = P(None, "row", "col")
    return jax.shard_map(body, mesh=mesh, in_specs=in_specs, out_specs=out_specs, check_vma=False)
```

profile of v0, /device:TPU:0, one launch (start us, length us, event | category | flops | bytes accessed | tf_op | source)
XLA Modules:
  0.0 267.1 jit_solution(11964594302407016854)
XLA Ops:
  6.5 0.0 all-gather.5.cloned.1.call-start
  6.5 0.7 broadcast_compare_fusion.2
  7.3 0.3 broadcast_in_dim.61
  7.6 0.1 copy.23
  7.7 0.7 broadcast_compare_fusion.1
  8.4 1.1 broadcast_select_fusion.1
  9.5 0.3 broadcast_in_dim.64
  9.9 1.0 fusion.6
  10.9 1.0 pad_maximum_fusion.1
  11.9 0.0 all-gather.5.cloned.1.call-update
  11.9 0.0 all-gather.7.cloned.1.call-start
  11.9 0.0 copy-done.4
  12.0 0.3 broadcast_in_dim.68
  12.3 0.1 copy.22
  12.4 0.9 broadcast_select_fusion
  13.2 0.0 all-gather.7.cloned.1.call-update
  13.3 0.0 all-gather.11.cloned.1.call-start
  13.3 0.7 all-gather.11.cloned.1.call-update
  14.0 0.0 all-gather.9.cloned.1.call-start
  14.1 29.2 %all-gather.5.cloned.1.call-done = bf16[3,256,2048]{2,1,0:T(8,128)(2,1)} async-done(((bf16[3,256,512]{2,1,0:T(8,128)(2,1)}), bf16[3,256,2048]{2,1,0:T(8,128)(2,1)}) %all-gather.5.cloned.1.call-update) | async-done | bytes 3145744 | tf_op jit(solution)/shard_map/all_gather | solution.py:38
  43.3 75.6 %all-gather.7.cloned.1.call-done = bf16[2,2048,512]{2,1,0:T(8,128)(2,1)} async-done(((bf16[2,256,512]{2,1,0:T(8,128)(2,1)}), bf16[2,2048,512]{2,1,0:T(8,128)(2,1)}) %all-gather.7.cloned.1.call-update) | async-done | bytes 4194320 | tf_op jit(solution)/shard_map/all_gather | solution.py:36
  118.9 3.9 %fusion.5 = bf16[2,256,512]{2,1,0:T(8,128)(2,1)S(1)} fusion(bf16[2,2048,512]{2,1,0:T(8,128)(2,1)} %all-gather.7.cloned.1.call-done, bf16[3,256,2048]{2,1,0:T(8,128)(2,1)} %all-gather.5.cloned.1.call-done), kind=kOutput, calls=%fused_computation.8 | convolution fusion | flops 1074003968 | bytes 5767168 | tf_op jit(solution)/shard_map/rl,slc->src/dot_general | solution.py:15
  122.8 0.0 copy-start.5
  122.8 1.3 convolution_convert_fusion
  124.1 1.1 pad_maximum_fusion
  125.2 0.0 all-gather.9.cloned.1.call-update
  125.2 0.3 broadcast_in_dim.58
  125.6 0.1 copy.24
  125.6 92.7 %all-gather.11.cloned.1.call-done = bf16[3,2048,512]{2,1,0:T(8,128)(2,1)} async-done(((bf16[3,256,512]{2,1,0:T(8,128)(2,1)}), bf16[3,2048,512]{2,1,0:T(8,128)(2,1)}) %all-gather.11.cloned.1.call-update) | async-done | bytes 6291472 | tf_op jit(solution)/shard_map/all_gather | solution.py:40
  218.4 34.1 %all-gather.9.cloned.1.call-done = bf16[4,256,2048]{2,1,0:T(8,128)(2,1)} async-done(((bf16[4,256,512]{2,1,0:T(8,128)(2,1)}), bf16[4,256,2048]{2,1,0:T(8,128)(2,1)}) %all-gather.9.cloned.1.call-update) | async-done | bytes 4194320 | tf_op jit(solution)/shard_map/all_gather | solution.py:42
  252.5 4.2 %fusion = f32[2,256,512]{2,1,0:T(8,128)S(1)} fusion(bf16[4,256,2048]{2,1,0:T(8,128)(2,1)} %all-gather.9.cloned.1.call-done, bf16[3,2048,512]{2,1,0:T(8,128)(2,1)} %all-gather.11.cloned.1.call-done), kind=kOutput, calls=%fused_computation | convolution fusion | flops 1073741824 | bytes 9437184 | tf_op jit(solution)/shard_map/srl,slc->src/dot_general | solution.py:23
  256.7 3.8 %fusion.4 = f32[2,256,512]{2,1,0:T(8,128)} fusion(f32[2,256,512]{2,1,0:T(8,128)S(1)} %fusion, bf16[4,256,2048]{2,1,0:T(8,128)(2,1)S(1)} %copy-done.2, bf16[3,2048,512]{2,1,0:T(8,128)(2,1)} %all-gather.11.cloned.1.call-done, pred[256,512]{1,0:T(8,128)(4,1)S(1)} %bitcast.52), kind=kOutput, calls=%fused_computation.5 | convolution fusion | flops 1074266112 | bytes 8519680 | tf_op jit(solution)/shard_map/srl,lc->src/dot_general | solution.py:20
  (16 shorter events, 0.1 us)
Async XLA Ops:
  6.5 5.4 %copy-start.4 = (s32[2,4]{1,0:T(2,128)S(1)}, s32[2,4]{1,0:T(2,128)}, u32[]{:S(2)}) copy-start(s32[2,4]{1,0:T(2,128)} %param.12) | copy-start | bytes 100
  6.5 5.9 %copy-start = (bf16[2,256,512]{2,1,0:T(8,128)(2,1)S(1)}, bf16[2,256,512]{2,1,0:T(8,128)(2,1)}, u32[]{:S(2)}) copy-start(bf16[2,256,512]{2,1,0:T(8,128)(2,1)} %param.9) | copy-start | bytes 1572868
  6.5 36.7 %all-gather.5.cloned.1.call-start = ((), (), s32[]{:S(2)}) async-start(), calls=%async_computation | async-start | bytes 3932160 | tf_op jit(solution)/shard_map/all_gather | solution.py:38
  11.9 107.0 %all-gather.7.cloned.1.call-start = ((), (), s32[]{:S(2)}) async-start(), calls=%async_computation.1 | async-start | bytes 4718592 | tf_op jit(solution)/shard_map/all_gather | solution.py:36
  13.3 205.1 %all-gather.11.cloned.1.call-start = ((), (), s32[]{:S(2)}) async-start(), calls=%async_computation.3 | async-start | bytes 7077888 | tf_op jit(solution)/shard_map/all_gather | solution.py:40
  14.0 238.5 %all-gather.9.cloned.1.call-start = ((), (), s32[]{:S(2)}) async-start(), calls=%async_computation.2 | async-start | bytes 5242880 | tf_op jit(solution)/shard_map/all_gather | solution.py:42
  43.3 79.5 %copy-start.3 = (bf16[3,256,2048]{2,1,0:T(8,128)(2,1)S(1)}, bf16[3,256,2048]{2,1,0:T(8,128)(2,1)}, u32[]{:S(2)}) copy-start(bf16[3,256,2048]{2,1,0:T(8,128)(2,1)} %all-gather.5.cloned.1.call-done) | copy-start | bytes 9437188
  118.9 3.9 %copy-start.1 = (bf16[2,2048,512]{2,1,0:T(8,128)(2,1)S(1)}, bf16[2,2048,512]{2,1,0:T(8,128)(2,1)}, u32[]{:S(2)}) copy-start(bf16[2,2048,512]{2,1,0:T(8,128)(2,1)} %all-gather.7.cloned.1.call-done) | copy-start | bytes 12582916
  122.8 2.4 copy-start.5
  252.5 4.2 %copy-start.2 = (bf16[4,256,2048]{2,1,0:T(8,128)(2,1)S(1)}, bf16[4,256,2048]{2,1,0:T(8,128)(2,1)}, u32[]{:S(2)}) copy-start(bf16[4,256,2048]{2,1,0:T(8,128)(2,1)} %all-gather.9.cloned.1.call-done) | copy-start | bytes 12582916
Sparse Core Ops, SparseCore 0:
  12.0 31.2 all-gather.4
  45.5 73.3 all-gather.6
  121.0 97.2 all-gather.10
  219.8 32.6 all-gather.8
where the time goes:
time: 267 us
  waiting for transfers between devices  232 us (87%)
  matrix products  13.3 us (5%)
  between operations  13.3 us (5%)
  other arithmetic  6.44 us (2%)
    all_gather x1, waiting for transfers between devices, body(): operator_cols = lax.all_gather(operators, 'row', axis=1, tiled=True)  92.7 us
    all_gather x1, waiting for transfers between devices, body(): density_cols = lax.all_gather(filtered, 'row', axis=1, tiled=True)  75.6 us
    all_gather x1, waiting for transfers between devices, body(): lax.all_gather(products, 'col', axis=2, tiled=True)  34.1 us
    all_gather x1, waiting for transfers between devices, body(): lax.all_gather(operators, 'col', axis=2, tiled=True)  29.2 us
  transfers between devices with their start and end apart: 4, of which 4 were waited for; matrix products, arithmetic and copies ran while one was open for 3% of the time, Pallas kernels for 0%

commit v1 on v0

--- a/solution.py
+++ b/solution.py
@@ -33,7 +33,12 @@
     smat = jnp.where(widen(metric_keep), basis_metric, jnp.zeros_like(basis_metric))
     filtered = jnp.where(widen(density_keep)[None], density, jnp.zeros_like(density))
     operators = jnp.concatenate([kohn_sham, smat[None]], axis=0)
-    density_cols = lax.all_gather(filtered, "row", axis=1, tiled=True)
+    ring = [filtered]
+    for hop in range(7):
+        ring.append(lax.ppermute(ring[-1], "row", [(dev, (dev + 1) % 8) for dev in range(8)]))
+    density_cols = jnp.roll(
+        jnp.concatenate(ring[::-1], axis=1), (lax.axis_index("row") + 1) * ring[0].shape[1], axis=1
+    )
     cols_part = density_cols
     products = first_terms(lax.all_gather(operators, "col", axis=2, tiled=True), cols_part)
     products = products.astype(jnp.bfloat16)

time: 267 us -> 283 us (1.060)
  local copies, waits for them, and re-layouts: 1.63 us -> 17.4 us
  waiting for transfers between devices: 232 us -> 223 us
  starting transfers between devices: 0.12 us -> 3.09 us
    ppermute x0 -> x7, waiting for transfers between devices: none -> 91.7 us  [body(): lax.ppermute(ring[-1], 'row', [(dev, (dev + 1) % 8) for dev in range(8)])]
    all_gather x1 -> x0, waiting for transfers between devices: 75.6 us -> none  [body(): density_cols = lax.all_gather(filtered, 'row', axis=1, tiled=True)]
    all_gather x1, waiting for transfers between devices: 29.2 us -> 0.01 us  [body(): lax.all_gather(operators, 'col', axis=2, tiled=True)]
    unnamed x15 -> x23, local copies, waits for them, and re-layouts: 0.23 us -> 16 us
    all_gather x1, waiting for transfers between devices: 92.7 us -> 101 us  [body(): operator_cols = lax.all_gather(operators, 'row', axis=1, tiled=True)]
    all_gather x1, waiting for transfers between devices: 34.1 us -> 29.8 us  [body(): lax.all_gather(products, 'col', axis=2, tiled=True)]
    ppermute x0 -> x7, starting transfers between devices: none -> 3.01 us  [body(): lax.ppermute(ring[-1], 'row', [(dev, (dev + 1) % 8) for dev in range(8)])]
  transfers between devices with their start and end apart: 4 -> 10, of which waited for: 4 -> 9; matrix products, arithmetic and copies ran while one was open for 3% -> 8% of each run, Pallas kernels for 0% -> 0%
where the time goes in v1:
time: 283 us; the launch traced here: 282 us
  waiting for transfers between devices  223 us (79%)
  local copies, waits for them, and re-layouts  17.4 us (6%)
  matrix products  15.9 us (6%)
  between operations  13.2 us (5%)
  other arithmetic  9.26 us (3%)
  starting transfers between devices  3.09 us (1%)
    all_gather x1, waiting for transfers between devices, body(): operator_cols = lax.all_gather(operators, 'row', axis=1, tiled=True)  101 us
    ppermute x7, waiting for transfers between devices, body(): lax.ppermute(ring[-1], 'row', [(dev, (dev + 1) % 8) for dev in range(8)])  91.7 us
    all_gather x1, waiting for transfers between devices, body(): lax.all_gather(products, 'col', axis=2, tiled=True)  29.8 us
    unnamed x23, local copies, waits for them, and re-layouts  16 us
  transfers between devices with their start and end apart: 10, of which 9 were waited for; matrix products, arithmetic and copies ran while one was open for 8% of the time, Pallas kernels for 0%

profile of v1, /device:TPU:0, one launch (start us, length us, event | category | flops | bytes accessed | tf_op | source)
XLA Modules:
  0.0 282.3 jit_solution(7701067807290225650)
XLA Ops:
  7.7 1.1 broadcast_select_fusion
  8.8 3.0 %collective-permute-start = (bf16[2,256,512]{2,1,0:T(8,128)(2,1)S(1)}, bf16[2,256,512]{2,1,0:T(8,128)(2,1)S(1)}, u32[]{:S(2)}, u32[]{:S(2)}) collective-permute-start(bf16[2,256,512]{2,1,0:T(8,128)(2,1)S(1)} %broadcast_select_fusion), channel_id=1, source_target_pairs={{0,4},{4,8},{8,12},{12,16},{16,20},{20,24},{24,28},{28,0},{1,5},{5... | collective-permute-start | bytes 1572872 | tf_op jit(solution)/shard_map/ppermute | solution.py:38
  11.8 15.0 %collective-permute-done = bf16[2,256,512]{2,1,0:T(8,128)(2,1)S(1)} collective-permute-done((bf16[2,256,512]{2,1,0:T(8,128)(2,1)S(1)}, bf16[2,256,512]{2,1,0:T(8,128)(2,1)S(1)}, u32[]{:S(2)}, u32[]{:S(2)}) %collective-permute-start) | collective-permute-done | bytes 524320 | tf_op jit(solution)/shard_map/ppermute | solution.py:38
  28.6 1.1 broadcast_select_fusion.1
  29.7 12.9 %collective-permute-done.1 = bf16[2,256,512]{2,1,0:T(8,128)(2,1)S(1)} collective-permute-done((bf16[2,256,512]{2,1,0:T(8,128)(2,1)S(1)}, bf16[2,256,512]{2,1,0:T(8,128)(2,1)S(1)}, u32[]{:S(2)}, u32[]{:S(2)}) %collective-permute-start.1) | collective-permute-done | bytes 524320 | tf_op jit(solution)/shard_map/ppermute | solution.py:38
  42.9 1.0 fusion.18
  44.0 1.0 pad_maximum_fusion.1
  45.0 12.5 %collective-permute-done.2 = bf16[2,256,512]{2,1,0:T(8,128)(2,1)S(1)} collective-permute-done((bf16[2,256,512]{2,1,0:T(8,128)(2,1)S(1)}, bf16[2,256,512]{2,1,0:T(8,128)(2,1)S(1)}, u32[]{:S(2)}, u32[]{:S(2)}) %collective-permute-start.2) | collective-permute-done | bytes 524320 | tf_op jit(solution)/shard_map/ppermute | solution.py:38
  57.5 14.0 %collective-permute-done.3 = bf16[2,256,512]{2,1,0:T(8,128)(2,1)S(1)} collective-permute-done((bf16[2,256,512]{2,1,0:T(8,128)(2,1)S(1)}, bf16[2,256,512]{2,1,0:T(8,128)(2,1)S(1)}, u32[]{:S(2)}, u32[]{:S(2)}) %collective-permute-start.3) | collective-permute-done | bytes 524320 | tf_op jit(solution)/shard_map/ppermute | solution.py:38
  71.4 13.0 %collective-permute-done.4 = bf16[2,256,512]{2,1,0:T(8,128)(2,1)S(1)} collective-permute-done((bf16[2,256,512]{2,1,0:T(8,128)(2,1)S(1)}, bf16[2,256,512]{2,1,0:T(8,128)(2,1)S(1)}, u32[]{:S(2)}, u32[]{:S(2)}) %collective-permute-start.4) | collective-permute-done | bytes 524320 | tf_op jit(solution)/shard_map/ppermute | solution.py:38
  84.5 12.2 %collective-permute-done.5 = bf16[2,256,512]{2,1,0:T(8,128)(2,1)} collective-permute-done((bf16[2,256,512]{2,1,0:T(8,128)(2,1)S(1)}, bf16[2,256,512]{2,1,0:T(8,128)(2,1)}, u32[]{:S(2)}, u32[]{:S(2)}) %collective-permute-start.5) | collective-permute-done | bytes 524320 | tf_op jit(solution)/shard_map/ppermute | solution.py:38
  96.7 12.2 %collective-permute-done.6 = bf16[2,256,512]{2,1,0:T(8,128)(2,1)} collective-permute-done((bf16[2,256,512]{2,1,0:T(8,128)(2,1)}, bf16[2,256,512]{2,1,0:T(8,128)(2,1)}, u32[]{:S(2)}, u32[]{:S(2)}) %collective-permute-start.6) | collective-permute-done | bytes 524320 | tf_op jit(solution)/shard_map/ppermute | solution.py:38
  108.9 1.9 constant_dynamic-update-slice_fusion.15
  110.8 1.8 constant_dynamic-update-slice_fusion.14
  113.4 0.8 constant_dynamic-update-slice_fusion.12
  114.3 0.8 constant_dynamic-update-slice_fusion.11
  115.1 0.8 constant_dynamic-update-slice_fusion.10
  115.9 0.8 constant_dynamic-update-slice_fusion.9
  116.8 0.9 constant_dynamic-update-slice_fusion.8
  117.7 1.9 constant_dynamic-update-slice_fusion.7
  119.6 1.9 constant_dynamic-update-slice_fusion.6
  121.4 0.8 constant_dynamic-update-slice_fusion.5
  123.9 0.8 constant_dynamic-update-slice_fusion.2
  124.7 0.9 constant_dynamic-update-slice_fusion.1
  125.6 1.0 constant_dynamic-update-slice_fusion
  126.6 4.1 %fusion.9 = bf16[2,256,512]{2,1,0:T(8,128)(2,1)S(1)} fusion(bf16[3,256,2048]{2,1,0:T(8,128)(2,1)} %all-gather.4.cloned.1.call-done, bf16[2,4096,512]{2,1,0:T(8,128)(2,1)} %constant_dynamic-update-slice_fusion, s32[]{:T(128)S(6)} %select_n.32), kind=kOutput, calls=%fused_computation.10 | convolution fusion | flops 1074003968 | bytes 7864324 | tf_op jit(solution)/shard_map/srl,slc->src/dot_general | solution.py:14
  130.7 3.8 %fusion.15 = bf16[2,256,512]{2,1,0:T(8,128)(2,1)S(1)} fusion(bf16[2,4096,512]{2,1,0:T(8,128)(2,1)} %constant_dynamic-update-slice_fusion, s32[]{:T(128)S(6)} %select_n.32, bf16[3,256,2048]{2,1,0:T(8,128)(2,1)} %all-gather.4.cloned.1.call-done), kind=kOutput, calls=%fused_computation.12 | convolution fusion | flops 1074003968 | bytes 5767172 | tf_op jit(solution)/shard_map/rl,slc->src/dot_general | solution.py:15
  134.4 1.1 pad_maximum_fusion
  136.7 29.8 %all-gather.6.cloned.1.call-done = bf16[4,256,2048]{2,1,0:T(8,128)(2,1)} async-done(((bf16[4,256,512]{2,1,0:T(8,128)(2,1)}), bf16[4,256,2048]{2,1,0:T(8,128)(2,1)}) %all-gather.6.cloned.1.call-update) | async-done | bytes 4194320 | tf_op jit(solution)/shard_map/all_gather | solution.py:47
  166.5 101.2 %all-gather.8.cloned.1.call-done = bf16[3,2048,512]{2,1,0:T(8,128)(2,1)} async-done(((bf16[3,256,512]{2,1,0:T(8,128)(2,1)}), bf16[3,2048,512]{2,1,0:T(8,128)(2,1)}) %all-gather.8.cloned.1.call-update) | async-done | bytes 6291472 | tf_op jit(solution)/shard_map/all_gather | solution.py:45
  267.7 4.2 %fusion = f32[2,256,512]{2,1,0:T(8,128)S(1)} fusion(bf16[4,256,2048]{2,1,0:T(8,128)(2,1)} %all-gather.6.cloned.1.call-done, bf16[3,2048,512]{2,1,0:T(8,128)(2,1)} %all-gather.8.cloned.1.call-done), kind=kOutput, calls=%fused_computation | convolution fusion | flops 1073741824 | bytes 9437184 | tf_op jit(solution)/shard_map/srl,slc->src/dot_general | solution.py:23
  271.9 3.8 %fusion.8 = f32[2,256,512]{2,1,0:T(8,128)} fusion(f32[2,256,512]{2,1,0:T(8,128)S(1)} %fusion, bf16[4,256,2048]{2,1,0:T(8,128)(2,1)S(1)} %copy-done.1, bf16[3,2048,512]{2,1,0:T(8,128)(2,1)} %all-gather.8.cloned.1.call-done, pred[256,512]{1,0:T(8,128)(4,1)S(1)} %bitcast.52), kind=kOutput, calls=%fused_computation.9 | convolution fusion | flops 1074266112 | bytes 8519680 | tf_op jit(solution)/shard_map/srl,lc->src/dot_general | solution.py:20
  (37 shorter events, 7.0 us)
Async XLA Ops:
  6.5 110.2 %copy-start = (bf16[2,256,512]{2,1,0:T(8,128)(2,1)S(1)}, bf16[2,256,512]{2,1,0:T(8,128)(2,1)}, u32[]{:S(2)}) copy-start(bf16[2,256,512]{2,1,0:T(8,128)(2,1)} %param.9) | copy-start | bytes 1572868
  6.5 120.0 %all-gather.4.cloned.1.call-start = ((), (), s32[]{:S(2)}) async-start(), calls=%async_computation | async-start | bytes 3932160 | tf_op jit(solution)/shard_map/all_gather | solution.py:43
  8.8 18.0 %collective-permute-start = (bf16[2,256,512]{2,1,0:T(8,128)(2,1)S(1)}, bf16[2,256,512]{2,1,0:T(8,128)(2,1)S(1)}, u32[]{:S(2)}, u32[]{:S(2)}) collective-permute-start(bf16[2,256,512]{2,1,0:T(8,128)(2,1)S(1)} %broadcast_select_fusion), channel_id=1, source_target_pairs={{0,4},{4,8},{8,12},{12,16},{16,20},{20,24},{24,28},{28,0},{1,5},{5... | collective-permute-start | bytes 1572872 | tf_op jit(solution)/shard_map/ppermute | solution.py:38
  26.8 15.8 %collective-permute-start.1 = (bf16[2,256,512]{2,1,0:T(8,128)(2,1)S(1)}, bf16[2,256,512]{2,1,0:T(8,128)(2,1)S(1)}, u32[]{:S(2)}, u32[]{:S(2)}) collective-permute-start(bf16[2,256,512]{2,1,0:T(8,128)(2,1)S(1)} %collective-permute-done), channel_id=1, source_target_pairs={{0,4},{4,8},{8,12},{12,16},{16,20},{20,24},{24,28},{28,0},{1,5},{5... | collective-permute-start | bytes 1572872 | tf_op jit(solution)/shard_map/ppermute | solution.py:38
  42.6 14.9 %collective-permute-start.2 = (bf16[2,256,512]{2,1,0:T(8,128)(2,1)S(1)}, bf16[2,256,512]{2,1,0:T(8,128)(2,1)S(1)}, u32[]{:S(2)}, u32[]{:S(2)}) collective-permute-start(bf16[2,256,512]{2,1,0:T(8,128)(2,1)S(1)} %collective-permute-done.1), channel_id=1, source_target_pairs={{0,4},{4,8},{8,12},{12,16},{16,20},{20,24},{24,28},{28,0},{1,5},{5... | collective-permute-start | bytes 1572872 | tf_op jit(solution)/shard_map/ppermute | solution.py:38
  45.0 121.5 %all-gather.6.cloned.1.call-start = ((), (), s32[]{:S(2)}) async-start(), calls=%async_computation.1 | async-start | bytes 5242880 | tf_op jit(solution)/shard_map/all_gather | solution.py:47
  57.5 14.0 %collective-permute-start.3 = (bf16[2,256,512]{2,1,0:T(8,128)(2,1)S(1)}, bf16[2,256,512]{2,1,0:T(8,128)(2,1)S(1)}, u32[]{:S(2)}, u32[]{:S(2)}) collective-permute-start(bf16[2,256,512]{2,1,0:T(8,128)(2,1)S(1)} %collective-permute-done.2), channel_id=1, source_target_pairs={{0,4},{4,8},{8,12},{12,16},{16,20},{20,24},{24,28},{28,0},{1,5},{5... | collective-permute-start | bytes 1572872 | tf_op jit(solution)/shard_map/ppermute | solution.py:38
  71.4 13.0 %collective-permute-start.4 = (bf16[2,256,512]{2,1,0:T(8,128)(2,1)S(1)}, bf16[2,256,512]{2,1,0:T(8,128)(2,1)S(1)}, u32[]{:S(2)}, u32[]{:S(2)}) collective-permute-start(bf16[2,256,512]{2,1,0:T(8,128)(2,1)S(1)} %collective-permute-done.3), channel_id=1, source_target_pairs={{0,4},{4,8},{8,12},{12,16},{16,20},{20,24},{24,28},{28,0},{1,5},{5... | collective-permute-start | bytes 1572872 | tf_op jit(solution)/shard_map/ppermute | solution.py:38
  84.5 12.2 %collective-permute-start.5 = (bf16[2,256,512]{2,1,0:T(8,128)(2,1)S(1)}, bf16[2,256,512]{2,1,0:T(8,128)(2,1)}, u32[]{:S(2)}, u32[]{:S(2)}) collective-permute-start(bf16[2,256,512]{2,1,0:T(8,128)(2,1)S(1)} %collective-permute-done.4), channel_id=1, source_target_pairs={{0,4},{4,8},{8,12},{12,16},{16,20},{20,24},{24,28},{28,0},{1,5},{5... | collective-permute-start | bytes 1572872 | tf_op jit(solution)/shard_map/ppermute | solution.py:38
  96.7 12.2 %collective-permute-start.6 = (bf16[2,256,512]{2,1,0:T(8,128)(2,1)}, bf16[2,256,512]{2,1,0:T(8,128)(2,1)}, u32[]{:S(2)}, u32[]{:S(2)}) collective-permute-start(bf16[2,256,512]{2,1,0:T(8,128)(2,1)} %collective-permute-done.5), channel_id=1, source_target_pairs={{0,4},{4,8},{8,12},{12,16},{16,20},{20,24},{24,28},{28,0},{1,5},{5... | collective-permute-start | bytes 1572872 | tf_op jit(solution)/shard_map/ppermute | solution.py:38
  130.6 5.6 %copy-start.2 = (s32[2,4]{1,0:T(2,128)S(1)}, s32[2,4]{1,0:T(2,128)}, u32[]{:S(2)}) copy-start(s32[2,4]{1,0:T(2,128)} %param.13) | copy-start | bytes 100
  135.5 132.2 %all-gather.8.cloned.1.call-start = ((), (), s32[]{:S(2)}) async-start(), calls=%async_computation.2 | async-start | bytes 7077888 | tf_op jit(solution)/shard_map/all_gather | solution.py:45
  267.7 4.2 %copy-start.1 = (bf16[4,256,2048]{2,1,0:T(8,128)(2,1)S(1)}, bf16[4,256,2048]{2,1,0:T(8,128)(2,1)}, u32[]{:S(2)}) copy-start(bf16[4,256,2048]{2,1,0:T(8,128)(2,1)} %all-gather.6.cloned.1.call-done) | copy-start | bytes 12582916
Sparse Core Ops, SparseCore 0:
  45.1 29.7 all-gather.3
  135.6 30.7 all-gather.5
  168.7 99.0 all-gather.7
